TPU v7x, 32 devices: a whole 2x2x4 slice. The times are simulated.
32 devices in a mesh: member: 8 (over z, x), space: 4 (over y, core).
Axes of the slice: x: 2, y: 2, z: 4, core: 2. Of those that a mesh axis runs over, the one named last changes fastest.
Arguments:
- states: float32 [1024, 24576], P('member', 'space'), may hold values from -6 to 6
- obs_values: float32 [2, 2048], replicated, may hold values from -6 to 6
- obs_weights: float32 [2, 2048], replicated, may hold values from 0.2 to 2
- obs_cell: int32 [2, 4, 4], P(None, 'space'), may hold values from 0 to 47
- op_select: int32 [2, 4, 4], P(None, 'space'), may hold values from 0 to 7
- op_table: float32 [8, 128, 128], replicated, may hold values from -0.5 to 0.5
- loc_obs: int32 [2, 4, 48, 8], P(None, 'space', 'member'), may hold values from 0 to 11
- loc_tile: int32 [2, 4, 48, 8], P(None, 'space', 'member'), may hold values from 0 to 7
- loc_tiles: float32 [8, 128, 128], replicated, may hold values from 0 to 1
Outputs:
- analysis: float32 [1024, 24576], P('member', 'space')
All inputs are finite; a program needn't handle non-finite values.
Results may differ from a plain program's by a relative error of at most 0.00012.
Values sent between devices are 32-bit elements; how exact they have to be, the bound alone decides.
A program may use at most 128 MiB of HBM per device.

v0:
```python
import jax
import jax.numpy as jnp
from jax import lax
from jax.sharding import PartitionSpec as P

K = 1024
BLK = 128
CB_DEV = 6
OB = 4


def with_halo(cells, sides, width):
    for axis, dim in sides:
        count = lax.axis_size(axis)
        head = lax.slice_in_dim(cells, 0, width, axis=dim)
        tail = lax.slice_in_dim(cells, cells.shape[dim] - width, cells.shape[dim], axis=dim)
        cells = jnp.concatenate(
            [
                lax.ppermute(tail, axis, [(i, (i + 1) % count) for i in range(count)]),
                cells,
                lax.ppermute(head, axis, [((i + 1) % count, i) for i in range(count)]),
            ],
            axis=dim,
        )
    return cells


def window_values(flat_row):
    space_n = lax.axis_size("space")
    slab_index = lax.axis_index("space")
    by_slab = flat_row.reshape(space_n, OB * BLK)
    slab_pick = (slab_index - 1 + jnp.arange(3, dtype=jnp.int32)) % space_n
    return by_slab[slab_pick].reshape(3 * OB * BLK)


def window(observed):
    return with_halo(observed, (("space", 1),), OB * BLK)


def prepare(window_obs, obs_values, obs_weights, batch_no):
    obs_mean = jnp.mean(window_obs, axis=0)
    obs_anom = window_obs - obs_mean
    values = window_values(obs_values[batch_no])
    weights = window_values(obs_weights[batch_no])
    innov = weights * (values - obs_mean) - 0.5 * weights * obs_anom
    return (obs_anom, innov)


def observe_members(ensemble, obs_cell, op_select, op_table, batch_no):
    blocks = ensemble.reshape(ensemble.shape[0], ensemble.shape[1] // BLK, BLK)
    picked = blocks[:, obs_cell[batch_no, 0]]
    operators = op_table[op_select[batch_no, 0]]
    observed = jnp.einsum("koc,opc->kop", picked, operators, precision=lax.Precision.HIGHEST)
    observed = observed.reshape(ensemble.shape[0], OB * BLK)
    return lax.all_gather(observed, "member", axis=0, tiled=True)


def observe_owners(cells, obs_cell, op_select, op_table, batch_no):
    member_index = lax.axis_index("member")
    cell_index = obs_cell[batch_no, 0]
    owned = cell_index // CB_DEV == member_index
    local_idx = cell_index % CB_DEV
    blocks = cells.reshape(K, CB_DEV, BLK)
    picked = blocks[:, local_idx]
    operators = op_table[op_select[batch_no, 0]]
    observed = jnp.einsum("koc,opc->kop", picked, operators, precision=lax.Precision.HIGHEST)
    observed = observed * owned.astype(jnp.float32)[None, :, None]
    return lax.psum(observed.reshape(K, OB * BLK), "member")


def to_cells(ensemble):
    return lax.all_to_all(ensemble, "member", split_axis=1, concat_axis=0, tiled=True)


def to_members(cells):
    return lax.all_to_all(cells, "member", split_axis=0, concat_axis=1, tiled=True)


def update_cells(cells, obs_anom, innov, loc_obs, loc_tile, loc_tiles, batch_no):
    blocks = cells.reshape(K, CB_DEV, BLK)
    state_mean = jnp.mean(blocks, axis=0)
    anom_win = obs_anom.reshape(K, 3 * OB, BLK)
    innov_win = innov.reshape(K, 3 * OB, BLK)

    def update_block(packed):
        cell_blk, mean_blk, reach, tile_pick = packed
        state_anom = cell_blk - mean_blk
        chosen = anom_win[:, reach]
        covariance = jnp.einsum(
            "kc,klo->lco", state_anom, chosen, precision=lax.Precision.HIGHEST
        ) / (K - 1)
        gain = loc_tiles[tile_pick] * covariance
        increment = jnp.einsum(
            "klo,lco->kc", innov_win[:, reach], gain, precision=lax.Precision.HIGHEST
        )
        return cell_blk + increment

    fresh = lax.map(
        update_block,
        (blocks.transpose(1, 0, 2), state_mean, loc_obs[batch_no, 0], loc_tile[batch_no, 0]),
    )
    return fresh.transpose(1, 0, 2).reshape(K, CB_DEV * BLK)


def per_device(
    states, obs_values, obs_weights, obs_cell, op_select, op_table, loc_obs, loc_tile, loc_tiles
):
    ensemble = states
    window_obs = window(observe_members(ensemble, obs_cell, op_select, op_table, 0))
    obs_anom, innov = prepare(window_obs, obs_values, obs_weights, 0)
    cells = to_cells(ensemble)
    cells = update_cells(cells, obs_anom, innov, loc_obs, loc_tile, loc_tiles, 0)
    window_obs = window(observe_owners(cells, obs_cell, op_select, op_table, 1))
    obs_anom, innov = prepare(window_obs, obs_values, obs_weights, 1)
    cells = update_cells(cells, obs_anom, innov, loc_obs, loc_tile, loc_tiles, 1)
    ensemble = to_members(cells)
    return ensemble


def solution(mesh):
    placed = (
        P("member", "space"),
        P(),
        P(),
        P(None, "space", None),
        P(None, "space", None),
        P(),
        P(None, "space", "member", None),
        P(None, "space", "member", None),
        P(),
    )
    return jax.shard_map(
        per_device, mesh=mesh, in_specs=placed, out_specs=P("member", "space"), check_vma=False
    )
```

profile of v0, /device:TPU:0, one launch (start us, length us, event | category | flops | bytes accessed | tf_op | source)
XLA Modules:
  0.0 793.8 jit_solution(15951240218992025015)
XLA Ops:
  18.9 7.3 all-to-all-start
  26.2 88.9 %all-gather.2.cloned.1.call-done = f32[1024,512]{0,1:T(8,128)} async-done(((f32[128,512]{0,1:T(8,128)}), f32[1024,512]{0,1:T(8,128)}) %all-gather.2.cloned.1.call-update) | async-done | bytes 2097168 | tf_op jit(solution)/shard_map/all_gather | solution.py:55
  122.3 5.4 copy.76
  134.5 27.0 %collective-permute-done = f32[1024,512]{0,1:T(8,128)} collective-permute-done((f32[1024,512]{0,1:T(8,128)}, f32[1024,512]{0,1:T(8,128)}, u32[]{:S(2)}, u32[]{:S(2)}) %collective-permute-start) | collective-permute-done | bytes 2097184 | tf_op jit(solution)/shard_map/ppermute | solution.py:19
  164.9 6.6 multiply_subtract_fusion.1
  171.5 6.5 copy.82
  178.1 6.6 copy.83
  186.5 169.5 %while.20 = (s32[]{:T(128)}, f32[6,1024,128]{2,1,0:T(8,128)}, f32[6,1024,128]{1,2,0:T(8,128)}, s32[6,8]{1,0:T(8,128)S(1)}, f32[1024,12,128]{2,0,1:T(8,128)}, /*i...) while((s32[]{:T(128)}, f32[6,1024,128]{2,1,0:T(8,128)}, ...), condition=%wide.region_3.4_spmd, body=%wide.region_2.3_spmd.sunk | while | flops 3221751808 | bytes 32516496 | solution.py:98
  186.5 5.6 gather_fusion.1
  194.3 8.5 %fusion.107 = f32[8,128,128]{1,2,0:T(8,128)S(1)} fusion(f32[8,128,128]{1,2,0:T(8,128)S(1)} %copy.108, f32[8,1024,128]{2,1,0:T(8,128)} %gather_fusion.1, f32[1,1024,128]{2,1,0:T(8,128)S(1)} %copy.109, f32[128]{0:T(128)S(1)} %fusion.106), kind=kOutput, calls=%fused_computation.20.clone.1 | convolution fusion | flops 1611005952 | bytes 5767680 | tf_op jit(solution)/shard_map/while/body/eval_jaxpr/kc,klo->lco/dot_general | solution.py:89
  202.7 5.6 gather_fusion.2
  208.4 6.4 fusion.108
  214.8 5.6 gather_fusion.1
  222.5 8.5 %fusion.107 = f32[8,128,128]{1,2,0:T(8,128)S(1)} fusion(f32[8,128,128]{1,2,0:T(8,128)S(1)} %copy.108, f32[8,1024,128]{2,1,0:T(8,128)} %gather_fusion.1, f32[1,1024,128]{2,1,0:T(8,128)S(1)} %copy.109, f32[128]{0:T(128)S(1)} %fusion.106), kind=kOutput, calls=%fused_computation.20.clone.1 | convolution fusion | flops 1611005952 | bytes 5767680 | tf_op jit(solution)/shard_map/while/body/eval_jaxpr/kc,klo->lco/dot_general | solution.py:89
  231.0 5.6 gather_fusion.2
  236.6 6.4 fusion.108
  243.0 5.6 gather_fusion.1
  250.8 8.5 %fusion.107 = f32[8,128,128]{1,2,0:T(8,128)S(1)} fusion(f32[8,128,128]{1,2,0:T(8,128)S(1)} %copy.108, f32[8,1024,128]{2,1,0:T(8,128)} %gather_fusion.1, f32[1,1024,128]{2,1,0:T(8,128)S(1)} %copy.109, f32[128]{0:T(128)S(1)} %fusion.106), kind=kOutput, calls=%fused_computation.20.clone.1 | convolution fusion | flops 1611005952 | bytes 5767680 | tf_op jit(solution)/shard_map/while/body/eval_jaxpr/kc,klo->lco/dot_general | solution.py:89
  259.2 5.6 gather_fusion.2
  264.9 6.4 fusion.108
  271.3 5.6 gather_fusion.1
  279.0 8.5 %fusion.107 = f32[8,128,128]{1,2,0:T(8,128)S(1)} fusion(f32[8,128,128]{1,2,0:T(8,128)S(1)} %copy.108, f32[8,1024,128]{2,1,0:T(8,128)} %gather_fusion.1, f32[1,1024,128]{2,1,0:T(8,128)S(1)} %copy.109, f32[128]{0:T(128)S(1)} %fusion.106), kind=kOutput, calls=%fused_computation.20.clone.1 | convolution fusion | flops 1611005952 | bytes 5767680 | tf_op jit(solution)/shard_map/while/body/eval_jaxpr/kc,klo->lco/dot_general | solution.py:89
  287.5 5.6 gather_fusion.2
  293.1 6.4 fusion.108
  299.6 5.6 gather_fusion.1
  307.3 8.5 %fusion.107 = f32[8,128,128]{1,2,0:T(8,128)S(1)} fusion(f32[8,128,128]{1,2,0:T(8,128)S(1)} %copy.108, f32[8,1024,128]{2,1,0:T(8,128)} %gather_fusion.1, f32[1,1024,128]{2,1,0:T(8,128)S(1)} %copy.109, f32[128]{0:T(128)S(1)} %fusion.106), kind=kOutput, calls=%fused_computation.20.clone.1 | convolution fusion | flops 1611005952 | bytes 5767680 | tf_op jit(solution)/shard_map/while/body/eval_jaxpr/kc,klo->lco/dot_general | solution.py:89
  315.8 5.6 gather_fusion.2
  321.4 6.4 fusion.108
  327.8 5.6 gather_fusion.1
  335.5 8.5 %fusion.107 = f32[8,128,128]{1,2,0:T(8,128)S(1)} fusion(f32[8,128,128]{1,2,0:T(8,128)S(1)} %copy.108, f32[8,1024,128]{2,1,0:T(8,128)} %gather_fusion.1, f32[1,1024,128]{2,1,0:T(8,128)S(1)} %copy.109, f32[128]{0:T(128)S(1)} %fusion.106), kind=kOutput, calls=%fused_computation.20.clone.1 | convolution fusion | flops 1611005952 | bytes 5767680 | tf_op jit(solution)/shard_map/while/body/eval_jaxpr/kc,klo->lco/dot_general | solution.py:89
  344.0 5.6 gather_fusion.2
  349.6 6.4 fusion.108
  359.9 4.8 fusion.68
  364.8 102.8 %all-reduce.2.cloned.1.call-done = f32[1024,512]{0,1:T(8,128)} async-done(((f32[1024,512]{0,1:T(8,128)}), f32[1024,512]{0,1:T(8,128)}) %all-reduce.2.cloned.1.call-update) | async-done | bytes 2097168 | tf_op jit(solution)/shard_map/psum | solution.py:68
  472.8 41.3 %collective-permute-done.2 = f32[1024,512]{0,1:T(8,128)} collective-permute-done((f32[1024,512]{0,1:T(8,128)}, f32[1024,512]{0,1:T(8,128)}, u32[]{:S(2)}, u32[]{:S(2)}) %collective-permute-start.2) | collective-permute-done | bytes 2097184 | tf_op jit(solution)/shard_map/ppermute | solution.py:19
  517.4 6.6 multiply_subtract_fusion
  524.0 6.6 copy.86
  530.6 6.5 copy.87
  539.0 162.1 %while.21 = (s32[]{:T(128)}, f32[6,1024,128]{2,1,0:T(8,128)}, f32[6,1024,128]{2,1,0:T(8,128)}, s32[6,8]{1,0:T(8,128)S(1)}, f32[1024,12,128]{2,0,1:T(8,128)}, /*i...) while((s32[]{:T(128)}, f32[6,1024,128]{2,1,0:T(8,128)}, ...), condition=%wide.region_8.9_spmd, body=%wide.region_7.8_spmd.sunk | while | flops 3221751808 | bytes 30419852 | solution.py:98
  539.0 5.5 gather_fusion.4
  545.4 8.6 %fusion.115 = f32[8,128,128]{1,2,0:T(8,128)S(1)} fusion(f32[8,128,128]{1,2,0:T(8,128)S(1)} %copy.110, f32[8,1024,128]{2,1,0:T(8,128)} %gather_fusion.4, f32[6,1024,128]{2,1,0:T(8,128)} %get-tuple-element.404, s32[]{:T(128)} %get-tuple-element.392, f32[128]{0:T(128)S(1)} %fusion.114), kind=kOutput, calls=%fused_computation.47.clone.1 | convolution fusion | flops 1611005952 | bytes 5768192 | tf_op jit(solution)/shard_map/while/body/eval_jaxpr/kc,klo->lco/dot_general | solution.py:89
  553.9 5.5 gather_fusion.5
  559.5 6.5 fusion.116
  566.0 5.5 gather_fusion.4
  572.4 8.6 %fusion.115 = f32[8,128,128]{1,2,0:T(8,128)S(1)} fusion(f32[8,128,128]{1,2,0:T(8,128)S(1)} %copy.110, f32[8,1024,128]{2,1,0:T(8,128)} %gather_fusion.4, f32[6,1024,128]{2,1,0:T(8,128)} %get-tuple-element.404, s32[]{:T(128)} %get-tuple-element.392, f32[128]{0:T(128)S(1)} %fusion.114), kind=kOutput, calls=%fused_computation.47.clone.1 | convolution fusion | flops 1611005952 | bytes 5768192 | tf_op jit(solution)/shard_map/while/body/eval_jaxpr/kc,klo->lco/dot_general | solution.py:89
  580.9 5.5 gather_fusion.5
  586.5 6.5 fusion.116
  593.0 5.5 gather_fusion.4
  599.4 8.6 %fusion.115 = f32[8,128,128]{1,2,0:T(8,128)S(1)} fusion(f32[8,128,128]{1,2,0:T(8,128)S(1)} %copy.110, f32[8,1024,128]{2,1,0:T(8,128)} %gather_fusion.4, f32[6,1024,128]{2,1,0:T(8,128)} %get-tuple-element.404, s32[]{:T(128)} %get-tuple-element.392, f32[128]{0:T(128)S(1)} %fusion.114), kind=kOutput, calls=%fused_computation.47.clone.1 | convolution fusion | flops 1611005952 | bytes 5768192 | tf_op jit(solution)/shard_map/while/body/eval_jaxpr/kc,klo->lco/dot_general | solution.py:89
  608.0 5.5 gather_fusion.5
  613.5 6.5 fusion.116
  620.0 5.5 gather_fusion.4
  626.4 8.6 %fusion.115 = f32[8,128,128]{1,2,0:T(8,128)S(1)} fusion(f32[8,128,128]{1,2,0:T(8,128)S(1)} %copy.110, f32[8,1024,128]{2,1,0:T(8,128)} %gather_fusion.4, f32[6,1024,128]{2,1,0:T(8,128)} %get-tuple-element.404, s32[]{:T(128)} %get-tuple-element.392, f32[128]{0:T(128)S(1)} %fusion.114), kind=kOutput, calls=%fused_computation.47.clone.1 | convolution fusion | flops 1611005952 | bytes 5768192 | tf_op jit(solution)/shard_map/while/body/eval_jaxpr/kc,klo->lco/dot_general | solution.py:89
  635.0 5.5 gather_fusion.5
  640.5 6.5 fusion.116
  647.1 5.5 gather_fusion.4
  653.4 8.6 %fusion.115 = f32[8,128,128]{1,2,0:T(8,128)S(1)} fusion(f32[8,128,128]{1,2,0:T(8,128)S(1)} %copy.110, f32[8,1024,128]{2,1,0:T(8,128)} %gather_fusion.4, f32[6,1024,128]{2,1,0:T(8,128)} %get-tuple-element.404, s32[]{:T(128)} %get-tuple-element.392, f32[128]{0:T(128)S(1)} %fusion.114), kind=kOutput, calls=%fused_computation.47.clone.1 | convolution fusion | flops 1611005952 | bytes 5768192 | tf_op jit(solution)/shard_map/while/body/eval_jaxpr/kc,klo->lco/dot_general | solution.py:89
  662.0 5.5 gather_fusion.5
  667.5 6.5 fusion.116
  674.1 5.5 gather_fusion.4
  680.4 8.6 %fusion.115 = f32[8,128,128]{1,2,0:T(8,128)S(1)} fusion(f32[8,128,128]{1,2,0:T(8,128)S(1)} %copy.110, f32[8,1024,128]{2,1,0:T(8,128)} %gather_fusion.4, f32[6,1024,128]{2,1,0:T(8,128)} %get-tuple-element.404, s32[]{:T(128)} %get-tuple-element.392, f32[128]{0:T(128)S(1)} %fusion.114), kind=kOutput, calls=%fused_computation.47.clone.1 | convolution fusion | flops 1611005952 | bytes 5768192 | tf_op jit(solution)/shard_map/while/body/eval_jaxpr/kc,klo->lco/dot_general | solution.py:89
  689.0 5.5 gather_fusion.5
  694.6 6.5 fusion.116
  707.9 75.6 %all_to_all.35 = f32[8,128,768]{1,2,0:T(8,128)} all-to-all(f32[8,128,768]{1,2,0:T(8,128)S(1)} %copy.89), channel_id=1, replica_groups=mesh['member'=8,'space'=4] {'member'}, dimensions={0} | all-to-all | bytes 6291456 | tf_op jit(solution)/shard_map/all_to_all | solution.py:76
  (165 shorter events, 73.1 us)
Async XLA Ops:
  6.5 10.3 %copy-start = (f32[8,128,128]{2,1,0:T(8,128)S(1)}, f32[8,128,128]{2,1,0:T(8,128)}, u32[]{:S(2)}) copy-start(f32[8,128,128]{2,1,0:T(8,128)} %param.18) | copy-start | bytes 1572868
  6.5 108.6 %all-gather.2.cloned.1.call-start = ((), (), s32[]{:S(2)}) async-start(), calls=%async_computation.2 | async-start | bytes 2359296 | tf_op jit(solution)/shard_map/all_gather | solution.py:55
  10.8 3.5 copy-start.9
  14.4 102.5 %copy-start.5 = (f32[2,2048]{1,0:T(2,128)S(1)}, f32[2,2048]{1,0:T(2,128)}, u32[]{:S(2)}) copy-start(f32[2,2048]{1,0:T(2,128)} %param.14) | copy-start | bytes 49156
  14.4 102.5 %copy-start.6 = (f32[2,2048]{1,0:T(2,128)S(1)}, f32[2,2048]{1,0:T(2,128)}, u32[]{:S(2)}) copy-start(f32[2,2048]{1,0:T(2,128)} %param.15) | copy-start | bytes 49156
  17.5 101.3 %copy-start.10 = (s32[2,1,4]{2,1,0:T(1,128)S(1)}, s32[2,1,4]{2,1,0:T(1,128)}, u32[]{:S(2)}) copy-start(s32[2,1,4]{2,1,0:T(1,128)} %param.16) | copy-start | bytes 100
  17.5 101.3 %copy-start.7 = (s32[2,1,6,8]{3,1,2,0:T(1,128)S(1)}, s32[2,1,6,8]{3,1,2,0:T(1,128)}, u32[]{:S(2)}) copy-start(s32[2,1,6,8]{3,1,2,0:T(1,128)} %param.20) | copy-start | bytes 1156
  17.5 101.3 %copy-start.8 = (s32[2,1,6,8]{3,1,2,0:T(1,128)S(1)}, s32[2,1,6,8]{3,1,2,0:T(1,128)}, u32[]{:S(2)}) copy-start(s32[2,1,6,8]{3,1,2,0:T(1,128)} %param.19) | copy-start | bytes 1156
  18.9 103.4 %all-to-all-start = ((f32[128,8,768]{0,2,1:T(8,128)}), f32[128,8,768]{0,2,1:T(8,128)}, u32[]{:S(2)}, u32[]{:S(2)}) async-start(f32[128,8,768]{0,2,1:T(8,128)} %bitcast.261), calls=%async_computation | async-start | bytes 6291456 | tf_op jit(solution)/shard_map/all_to_all | solution.py:72
  26.2 441.4 %all-reduce.2.cloned.1.call-start = ((), (), s32[]{:S(2)}) async-start(), calls=%async_computation.3 | async-start | bytes 4194304 | tf_op jit(solution)/shard_map/psum | solution.py:68
  115.1 46.4 %collective-permute-start = (f32[1024,512]{0,1:T(8,128)}, f32[1024,512]{0,1:T(8,128)}, u32[]{:S(2)}, u32[]{:S(2)}) collective-permute-start(f32[1024,512]{0,1:T(8,128)} %all-gather.2.cloned.1.call-done), channel_id=1, source_target_pairs={{0,1},{1,2},{2,3},{3,0},{4,5},{5,6},{6,7},{7,4},{8,9},{9,10},{10,1... | collective-permute-start | bytes 6291464 | tf_op jit(solution)/shard_map/ppermute | solution.py:19
  115.1 47.3 %collective-permute-start.1 = (f32[1024,512]{0,1:T(8,128)}, f32[1024,512]{0,1:T(8,128)}, u32[]{:S(2)}, u32[]{:S(2)}) collective-permute-start(f32[1024,512]{0,1:T(8,128)} %all-gather.2.cloned.1.call-done), channel_id=1, source_target_pairs={{1,0},{2,1},{3,2},{0,3},{5,4},{6,5},{7,6},{4,7},{9,8},{10,9},{11,1... | collective-permute-start | bytes 6291464 | tf_op jit(solution)/shard_map/ppermute | solution.py:21
  127.7 34.7 %copy-start.3 = (f32[1024,512]{0,1:T(8,128)S(1)}, f32[1024,512]{0,1:T(8,128)}, u32[]{:S(2)}) copy-start(f32[1024,512]{0,1:T(8,128)} %all-gather.2.cloned.1.call-done) | copy-start | bytes 6291460
  178.1 8.4 %copy-start.2 = (f32[8,128,128]{2,1,0:T(8,128)S(1)}, f32[8,128,128]{2,1,0:T(8,128)}, u32[]{:S(2)}) copy-start(f32[8,128,128]{2,1,0:T(8,128)} %param.21) | copy-start | bytes 1572868
  467.6 46.5 %collective-permute-start.2 = (f32[1024,512]{0,1:T(8,128)}, f32[1024,512]{0,1:T(8,128)}, u32[]{:S(2)}, u32[]{:S(2)}) collective-permute-start(f32[1024,512]{0,1:T(8,128)} %all-reduce.2.cloned.1.call-done), channel_id=1, source_target_pairs={{0,1},{1,2},{2,3},{3,0},{4,5},{5,6},{6,7},{7,4},{8,9},{9,10},{10,1... | collective-permute-start | bytes 6291464 | tf_op jit(solution)/shard_map/ppermute | solution.py:19
  467.6 47.2 %collective-permute-start.3 = (f32[1024,512]{0,1:T(8,128)}, f32[1024,512]{0,1:T(8,128)}, u32[]{:S(2)}, u32[]{:S(2)}) collective-permute-start(f32[1024,512]{0,1:T(8,128)} %all-reduce.2.cloned.1.call-done), channel_id=1, source_target_pairs={{1,0},{2,1},{3,2},{0,3},{5,4},{6,5},{7,6},{4,7},{9,8},{10,9},{11,1... | collective-permute-start | bytes 6291464 | tf_op jit(solution)/shard_map/ppermute | solution.py:21
  470.5 44.3 %copy-start.4 = (f32[1024,512]{0,1:T(8,128)S(1)}, f32[1024,512]{0,1:T(8,128)}, u32[]{:S(2)}) copy-start(f32[1024,512]{0,1:T(8,128)} %all-reduce.2.cloned.1.call-done) | copy-start | bytes 6291460
  707.8 79.1 %copy-start.1 = (f32[8,128,128]{2,1,0:T(8,128)S(1)}, f32[8,128,128]{2,1,0:T(8,128)}, u32[]{:S(2)}) copy-start(f32[8,128,128]{2,1,0:T(8,128)} %param.18) | copy-start | bytes 1572868
Sparse Core Ops, SparseCore 0:
  19.0 96.0 all-gather.1
  364.9 102.6 all-reduce.1
where the time goes:
time: 796 us; the launch traced here: 794 us
  waiting for transfers between devices  265 us (33%)
  local copies, waits for them, and re-layouts  219 us (28%)
  matrix products  186 us (23%)
  blocking collectives  75.6 us (9%)
  other arithmetic  23.5 us (3%)
  between operations  13.7 us (2%)
  starting transfers between devices  10.8 us (1%)
    psum x1, waiting for transfers between devices, observe_owners(): return lax.psum(observed.reshape(K, OB * BLK), 'member')  103 us
    dot_general x12, matrix products, update_block(): jnp.einsum('kc,klo->lco', state_anom, chosen, precision=lax.Precision.HIG...  102 us
    all_gather x1, waiting for transfers between devices, observe_members(): return lax.all_gather(observed, 'member', axis=0, tiled=True)  88.9 us
    dot_general x12, matrix products, update_block(): jnp.einsum('klo,lco->kc', innov_win[:, reach], gain, precision=lax.Precis...  77.6 us
    all_to_all x1, blocking collectives, to_members(): lax.all_to_all(cells, 'member', split_axis=0, concat_axis=1, tiled=True)  75.6 us
    ppermute x2, waiting for transfers between devices, with_halo(): lax.ppermute(tail, axis, [(i, (i + 1) % count) for i in range(count)])  68.4 us
    gather x12, local copies, waits for them, and re-layouts, update_block(): innov_win[:, reach]  67 us
    gather x12, local copies, waits for them, and re-layouts, update_block(): chosen = anom_win[:, reach]  67 us
  transfers between devices with their start and end apart: 7, of which 7 were waited for; matrix products, arithmetic and copies ran while one was open for 2% of the time, Pallas kernels for 0%

commit v1 on v0

--- a/solution.py
+++ b/solution.py
@@ -52,7 +52,9 @@
     operators = op_table[op_select[batch_no, 0]]
     observed = jnp.einsum("koc,opc->kop", picked, operators, precision=lax.Precision.HIGHEST)
     observed = observed.reshape(ensemble.shape[0], OB * BLK)
-    return lax.all_gather(observed, "member", axis=0, tiled=True)
+    return jnp.concatenate(
+        lax.all_to_all(jnp.stack([observed] * lax.axis_size("member")), "member", 0, 0), axis=0
+    )
 
 
 def observe_owners(cells, obs_cell, op_select, op_table, batch_no):

time: 796 us -> 792 us (level)
  waiting for transfers between devices: 265 us -> 204 us
  blocking collectives: 75.6 us -> 131 us
    all_gather x1 -> x0, waiting for transfers between devices: 88.9 us -> none  [observe_members(): return lax.all_gather(observed, 'member', axis=0, tiled=True)]
    all_to_all x1, waiting for transfers between devices: 3.47 us -> 60.1 us  [to_cells(): lax.all_to_all(ensemble, 'member', split_axis=1, concat_axis=0, tiled=True)]
    all_to_all x0 -> x1, blocking collectives: none -> 55.3 us  [observe_members(): lax.all_to_all(jnp.stack([observed] * lax.axis_size('member')), 'member',...]
    ppermute x2, waiting for transfers between devices: 68.4 us -> 41.3 us  [with_halo(): lax.ppermute(tail, axis, [(i, (i + 1) % count) for i in range(count)])]
  transfers between devices with their start and end apart: 7 -> 6, of which waited for: 7 -> 4; matrix products, arithmetic and copies ran while one was open for 2% -> 3% of each run, Pallas kernels for 0% -> 0%
where the time goes in v1:
time: 792 us; the launch traced here: 789 us
  local copies, waits for them, and re-layouts  223 us (28%)
  waiting for transfers between devices  204 us (26%)
  matrix products  185 us (23%)
  blocking collectives  131 us (17%)
  other arithmetic  24.1 us (3%)
  between operations  13.7 us (2%)
  starting transfers between devices  8.11 us (1%)
    dot_general x12, matrix products, update_block(): jnp.einsum('kc,klo->lco', state_anom, chosen, precision=lax.Precision.HIG...  102 us
    psum x1, waiting for transfers between devices, observe_owners(): return lax.psum(observed.reshape(K, OB * BLK), 'member')  102 us
    dot_general x12, matrix products, update_block(): jnp.einsum('klo,lco->kc', innov_win[:, reach], gain, precision=lax.Precis...  77.6 us
    all_to_all x1, blocking collectives, to_members(): lax.all_to_all(cells, 'member', split_axis=0, concat_axis=1, tiled=True)  75.6 us
    gather x12, local copies, waits for them, and re-layouts, update_block(): innov_win[:, reach]  66.3 us
    gather x12, local copies, waits for them, and re-layouts, update_block(): chosen = anom_win[:, reach]  66.3 us
    all_to_all x1, waiting for transfers between devices, to_cells(): lax.all_to_all(ensemble, 'member', split_axis=1, concat_axis=0, tiled=True)  60.1 us
    all_to_all x1, blocking collectives, observe_members(): lax.all_to_all(jnp.stack([observed] * lax.axis_size('member')), 'member',...  55.3 us
  transfers between devices with their start and end apart: 6, of which 4 were waited for; matrix products, arithmetic and copies ran while one was open for 3% of the time, Pallas kernels for 0%

profile of v1, /device:TPU:0, one launch (start us, length us, event | category | flops | bytes accessed | tf_op | source)
XLA Modules:
  0.0 789.3 jit_solution(3340478874945987645)
XLA Ops:
  18.2 55.3 %all_to_all.40 = f32[8,128,512]{1,2,0:T(8,128)S(1)} all-to-all(f32[8,128,512]{1,2,0:T(8,128)S(1)} %stack.3), channel_id=1, replica_groups=mesh['member'=8,'space'=4] {'member'}, dimensions={0} | all-to-all | bytes 4194304 | tf_op jit(solution)/shard_map/all_to_all | solution.py:56
  73.6 4.6 all-to-all-start
  87.9 60.1 %all-to-all-done = f32[128,8,768]{0,2,1:T(8,128)} async-done(((f32[128,8,768]{0,2,1:T(8,128)}), f32[128,8,768]{0,2,1:T(8,128)}, u32[]{:S(2)}, u32[]{:S(2)}) %all-to-all-start) | async-done | bytes 3145760 | tf_op jit(solution)/shard_map/all_to_all | solution.py:74
  148.0 5.4 copy.75
  163.1 6.6 multiply_subtract_fusion.1
  169.7 6.6 copy.83
  176.3 6.6 copy.84
  184.8 168.4 %while.20 = (s32[]{:T(128)}, f32[6,1024,128]{2,1,0:T(8,128)}, f32[6,1024,128]{1,2,0:T(8,128)}, s32[6,8]{1,0:T(8,128)S(1)}, f32[1024,12,128]{2,0,1:T(8,128)}, /*i...) while((s32[]{:T(128)}, f32[6,1024,128]{2,1,0:T(8,128)}, ...), condition=%wide.region_3.4_spmd, body=%wide.region_2.3_spmd.sunk | while | flops 3221751808 | bytes 32516496 | solution.py:100
  184.8 5.5 gather_fusion.1
  192.4 8.5 %fusion.108 = f32[8,128,128]{1,2,0:T(8,128)S(1)} fusion(f32[8,128,128]{1,2,0:T(8,128)S(1)} %copy.111, f32[8,1024,128]{2,1,0:T(8,128)} %gather_fusion.1, f32[1,1024,128]{2,1,0:T(8,128)S(1)} %copy.112, f32[128]{0:T(128)S(1)} %fusion.107), kind=kOutput, calls=%fused_computation.20.clone.1 | convolution fusion | flops 1611005952 | bytes 5767680 | tf_op jit(solution)/shard_map/while/body/eval_jaxpr/kc,klo->lco/dot_general | solution.py:91
  200.9 5.5 gather_fusion.2
  206.4 6.4 fusion.109
  212.9 5.5 gather_fusion.1
  220.5 8.5 %fusion.108 = f32[8,128,128]{1,2,0:T(8,128)S(1)} fusion(f32[8,128,128]{1,2,0:T(8,128)S(1)} %copy.111, f32[8,1024,128]{2,1,0:T(8,128)} %gather_fusion.1, f32[1,1024,128]{2,1,0:T(8,128)S(1)} %copy.112, f32[128]{0:T(128)S(1)} %fusion.107), kind=kOutput, calls=%fused_computation.20.clone.1 | convolution fusion | flops 1611005952 | bytes 5767680 | tf_op jit(solution)/shard_map/while/body/eval_jaxpr/kc,klo->lco/dot_general | solution.py:91
  229.0 5.5 gather_fusion.2
  234.5 6.4 fusion.109
  240.9 5.5 gather_fusion.1
  248.5 8.5 %fusion.108 = f32[8,128,128]{1,2,0:T(8,128)S(1)} fusion(f32[8,128,128]{1,2,0:T(8,128)S(1)} %copy.111, f32[8,1024,128]{2,1,0:T(8,128)} %gather_fusion.1, f32[1,1024,128]{2,1,0:T(8,128)S(1)} %copy.112, f32[128]{0:T(128)S(1)} %fusion.107), kind=kOutput, calls=%fused_computation.20.clone.1 | convolution fusion | flops 1611005952 | bytes 5767680 | tf_op jit(solution)/shard_map/while/body/eval_jaxpr/kc,klo->lco/dot_general | solution.py:91
  257.0 5.5 gather_fusion.2
  262.5 6.4 fusion.109
  269.0 5.5 gather_fusion.1
  276.6 8.5 %fusion.108 = f32[8,128,128]{1,2,0:T(8,128)S(1)} fusion(f32[8,128,128]{1,2,0:T(8,128)S(1)} %copy.111, f32[8,1024,128]{2,1,0:T(8,128)} %gather_fusion.1, f32[1,1024,128]{2,1,0:T(8,128)S(1)} %copy.112, f32[128]{0:T(128)S(1)} %fusion.107), kind=kOutput, calls=%fused_computation.20.clone.1 | convolution fusion | flops 1611005952 | bytes 5767680 | tf_op jit(solution)/shard_map/while/body/eval_jaxpr/kc,klo->lco/dot_general | solution.py:91
  285.1 5.5 gather_fusion.2
  290.6 6.4 fusion.109
  297.1 5.5 gather_fusion.1
  304.7 8.5 %fusion.108 = f32[8,128,128]{1,2,0:T(8,128)S(1)} fusion(f32[8,128,128]{1,2,0:T(8,128)S(1)} %copy.111, f32[8,1024,128]{2,1,0:T(8,128)} %gather_fusion.1, f32[1,1024,128]{2,1,0:T(8,128)S(1)} %copy.112, f32[128]{0:T(128)S(1)} %fusion.107), kind=kOutput, calls=%fused_computation.20.clone.1 | convolution fusion | flops 1611005952 | bytes 5767680 | tf_op jit(solution)/shard_map/while/body/eval_jaxpr/kc,klo->lco/dot_general | solution.py:91
  313.2 5.5 gather_fusion.2
  318.7 6.4 fusion.109
  325.1 5.5 gather_fusion.1
  332.7 8.5 %fusion.108 = f32[8,128,128]{1,2,0:T(8,128)S(1)} fusion(f32[8,128,128]{1,2,0:T(8,128)S(1)} %copy.111, f32[8,1024,128]{2,1,0:T(8,128)} %gather_fusion.1, f32[1,1024,128]{2,1,0:T(8,128)S(1)} %copy.112, f32[128]{0:T(128)S(1)} %fusion.107), kind=kOutput, calls=%fused_computation.20.clone.1 | convolution fusion | flops 1611005952 | bytes 5767680 | tf_op jit(solution)/shard_map/while/body/eval_jaxpr/kc,klo->lco/dot_general | solution.py:91
  341.2 5.5 gather_fusion.2
  346.7 6.5 fusion.109
  357.1 4.8 fusion.68
  361.9 101.5 %all-reduce.2.cloned.1.call-done = f32[1024,512]{0,1:T(8,128)} async-done(((f32[1024,512]{0,1:T(8,128)}), f32[1024,512]{0,1:T(8,128)}) %all-reduce.2.cloned.1.call-update) | async-done | bytes 2097168 | tf_op jit(solution)/shard_map/psum | solution.py:70
  468.6 41.3 %collective-permute-done.2 = f32[1024,512]{0,1:T(8,128)} collective-permute-done((f32[1024,512]{0,1:T(8,128)}, f32[1024,512]{0,1:T(8,128)}, u32[]{:S(2)}, u32[]{:S(2)}) %collective-permute-start.2) | collective-permute-done | bytes 2097184 | tf_op jit(solution)/shard_map/ppermute | solution.py:19
  513.2 6.6 multiply_subtract_fusion
  519.7 6.6 copy.87
  526.3 6.6 copy.88
  534.7 161.8 %while.21 = (s32[]{:T(128)}, f32[6,1024,128]{2,1,0:T(8,128)}, f32[6,1024,128]{2,1,0:T(8,128)}, s32[6,8]{1,0:T(8,128)S(1)}, f32[1024,12,128]{2,0,1:T(8,128)}, /*i...) while((s32[]{:T(128)}, f32[6,1024,128]{2,1,0:T(8,128)}, ...), condition=%wide.region_8.9_spmd, body=%wide.region_7.8_spmd.sunk | while | flops 3221751808 | bytes 30419852 | solution.py:100
  534.8 5.5 gather_fusion.4
  541.1 8.6 %fusion.116 = f32[8,128,128]{1,2,0:T(8,128)S(1)} fusion(f32[8,128,128]{1,2,0:T(8,128)S(1)} %copy.113, f32[8,1024,128]{2,1,0:T(8,128)} %gather_fusion.4, f32[6,1024,128]{2,1,0:T(8,128)} %get-tuple-element.404, s32[]{:T(128)} %get-tuple-element.392, f32[128]{0:T(128)S(1)} %fusion.115), kind=kOutput, calls=%fused_computation.47.clone.1 | convolution fusion | flops 1611005952 | bytes 5768192 | tf_op jit(solution)/shard_map/while/body/eval_jaxpr/kc,klo->lco/dot_general | solution.py:91
  549.7 5.5 gather_fusion.5
  555.2 6.5 fusion.117
  561.7 5.5 gather_fusion.4
  568.1 8.6 %fusion.116 = f32[8,128,128]{1,2,0:T(8,128)S(1)} fusion(f32[8,128,128]{1,2,0:T(8,128)S(1)} %copy.113, f32[8,1024,128]{2,1,0:T(8,128)} %gather_fusion.4, f32[6,1024,128]{2,1,0:T(8,128)} %get-tuple-element.404, s32[]{:T(128)} %get-tuple-element.392, f32[128]{0:T(128)S(1)} %fusion.115), kind=kOutput, calls=%fused_computation.47.clone.1 | convolution fusion | flops 1611005952 | bytes 5768192 | tf_op jit(solution)/shard_map/while/body/eval_jaxpr/kc,klo->lco/dot_general | solution.py:91
  576.6 5.5 gather_fusion.5
  582.2 6.5 fusion.117
  588.7 5.5 gather_fusion.4
  595.0 8.6 %fusion.116 = f32[8,128,128]{1,2,0:T(8,128)S(1)} fusion(f32[8,128,128]{1,2,0:T(8,128)S(1)} %copy.113, f32[8,1024,128]{2,1,0:T(8,128)} %gather_fusion.4, f32[6,1024,128]{2,1,0:T(8,128)} %get-tuple-element.404, s32[]{:T(128)} %get-tuple-element.392, f32[128]{0:T(128)S(1)} %fusion.115), kind=kOutput, calls=%fused_computation.47.clone.1 | convolution fusion | flops 1611005952 | bytes 5768192 | tf_op jit(solution)/shard_map/while/body/eval_jaxpr/kc,klo->lco/dot_general | solution.py:91
  603.6 5.5 gather_fusion.5
  609.1 6.5 fusion.117
  615.7 5.5 gather_fusion.4
  622.0 8.6 %fusion.116 = f32[8,128,128]{1,2,0:T(8,128)S(1)} fusion(f32[8,128,128]{1,2,0:T(8,128)S(1)} %copy.113, f32[8,1024,128]{2,1,0:T(8,128)} %gather_fusion.4, f32[6,1024,128]{2,1,0:T(8,128)} %get-tuple-element.404, s32[]{:T(128)} %get-tuple-element.392, f32[128]{0:T(128)S(1)} %fusion.115), kind=kOutput, calls=%fused_computation.47.clone.1 | convolution fusion | flops 1611005952 | bytes 5768192 | tf_op jit(solution)/shard_map/while/body/eval_jaxpr/kc,klo->lco/dot_general | solution.py:91
  630.6 5.5 gather_fusion.5
  636.1 6.5 fusion.117
  642.7 5.5 gather_fusion.4
  649.0 8.6 %fusion.116 = f32[8,128,128]{1,2,0:T(8,128)S(1)} fusion(f32[8,128,128]{1,2,0:T(8,128)S(1)} %copy.113, f32[8,1024,128]{2,1,0:T(8,128)} %gather_fusion.4, f32[6,1024,128]{2,1,0:T(8,128)} %get-tuple-element.404, s32[]{:T(128)} %get-tuple-element.392, f32[128]{0:T(128)S(1)} %fusion.115), kind=kOutput, calls=%fused_computation.47.clone.1 | convolution fusion | flops 1611005952 | bytes 5768192 | tf_op jit(solution)/shard_map/while/body/eval_jaxpr/kc,klo->lco/dot_general | solution.py:91
  657.6 5.5 gather_fusion.5
  663.1 6.5 fusion.117
  669.6 5.5 gather_fusion.4
  676.0 8.6 %fusion.116 = f32[8,128,128]{1,2,0:T(8,128)S(1)} fusion(f32[8,128,128]{1,2,0:T(8,128)S(1)} %copy.113, f32[8,1024,128]{2,1,0:T(8,128)} %gather_fusion.4, f32[6,1024,128]{2,1,0:T(8,128)} %get-tuple-element.404, s32[]{:T(128)} %get-tuple-element.392, f32[128]{0:T(128)S(1)} %fusion.115), kind=kOutput, calls=%fused_computation.47.clone.1 | convolution fusion | flops 1611005952 | bytes 5768192 | tf_op jit(solution)/shard_map/while/body/eval_jaxpr/kc,klo->lco/dot_general | solution.py:91
  684.5 5.5 gather_fusion.5
  690.1 6.5 fusion.117
  703.4 75.6 %all_to_all.41 = f32[8,128,768]{1,2,0:T(8,128)} all-to-all(f32[8,128,768]{1,2,0:T(8,128)S(1)} %copy.90), channel_id=1, replica_groups=mesh['member'=8,'space'=4] {'member'}, dimensions={0} | all-to-all | bytes 6291456 | tf_op jit(solution)/shard_map/all_to_all | solution.py:78
  (165 shorter events, 74.6 us)
Async XLA Ops:
  6.5 10.3 %copy-start = (f32[8,128,128]{2,1,0:T(8,128)S(1)}, f32[8,128,128]{2,1,0:T(8,128)}, u32[]{:S(2)}) copy-start(f32[8,128,128]{2,1,0:T(8,128)} %param.18) | copy-start | bytes 1572868
  10.8 3.5 copy-start.8
  73.6 8.0 %copy-start.4 = (f32[2,2048]{1,0:T(2,128)S(1)}, f32[2,2048]{1,0:T(2,128)}, u32[]{:S(2)}) copy-start(f32[2,2048]{1,0:T(2,128)} %param.14) | copy-start | bytes 49156
  73.6 8.0 %copy-start.5 = (f32[2,2048]{1,0:T(2,128)S(1)}, f32[2,2048]{1,0:T(2,128)}, u32[]{:S(2)}) copy-start(f32[2,2048]{1,0:T(2,128)} %param.15) | copy-start | bytes 49156
  73.6 9.9 %copy-start.9 = (s32[2,1,4]{2,1,0:T(1,128)S(1)}, s32[2,1,4]{2,1,0:T(1,128)}, u32[]{:S(2)}) copy-start(s32[2,1,4]{2,1,0:T(1,128)} %param.16) | copy-start | bytes 100
  73.6 9.9 %copy-start.6 = (s32[2,1,6,8]{3,1,2,0:T(1,128)S(1)}, s32[2,1,6,8]{3,1,2,0:T(1,128)}, u32[]{:S(2)}) copy-start(s32[2,1,6,8]{3,1,2,0:T(1,128)} %param.20) | copy-start | bytes 1156
  73.6 10.0 %copy-start.7 = (s32[2,1,6,8]{3,1,2,0:T(1,128)S(1)}, s32[2,1,6,8]{3,1,2,0:T(1,128)}, u32[]{:S(2)}) copy-start(s32[2,1,6,8]{3,1,2,0:T(1,128)} %param.19) | copy-start | bytes 1156
  73.6 74.4 %all-to-all-start = ((f32[128,8,768]{0,2,1:T(8,128)}), f32[128,8,768]{0,2,1:T(8,128)}, u32[]{:S(2)}, u32[]{:S(2)}) async-start(f32[128,8,768]{0,2,1:T(8,128)} %bitcast.267), calls=%async_computation | async-start | bytes 6291456 | tf_op jit(solution)/shard_map/all_to_all | solution.py:74
  78.2 385.3 %all-reduce.2.cloned.1.call-start = ((), (), s32[]{:S(2)}) async-start(), calls=%async_computation.3 | async-start | bytes 4194304 | tf_op jit(solution)/shard_map/psum | solution.py:70
  79.8 80.2 %collective-permute-start = (f32[1024,512]{0,1:T(8,128)}, f32[1024,512]{0,1:T(8,128)}, u32[]{:S(2)}, u32[]{:S(2)}) collective-permute-start(f32[1024,512]{0,1:T(8,128)} %copy_bitcast_fusion), channel_id=1, source_target_pairs={{0,1},{1,2},{2,3},{3,0},{4,5},{5,6},{6,7},{7,4},{8,9},{9,10},{10,1... | collective-permute-start | bytes 6291464 | tf_op jit(solution)/shard_map/ppermute | solution.py:19
  79.8 80.2 %collective-permute-start.1 = (f32[1024,512]{0,1:T(8,128)}, f32[1024,512]{0,1:T(8,128)}, u32[]{:S(2)}, u32[]{:S(2)}) collective-permute-start(f32[1024,512]{0,1:T(8,128)} %copy_bitcast_fusion), channel_id=1, source_target_pairs={{1,0},{2,1},{3,2},{0,3},{5,4},{6,5},{7,6},{4,7},{9,8},{10,9},{11,1... | collective-permute-start | bytes 6291464 | tf_op jit(solution)/shard_map/ppermute | solution.py:21
  176.3 8.5 %copy-start.2 = (f32[8,128,128]{2,1,0:T(8,128)S(1)}, f32[8,128,128]{2,1,0:T(8,128)}, u32[]{:S(2)}) copy-start(f32[8,128,128]{2,1,0:T(8,128)} %param.21) | copy-start | bytes 1572868
  463.4 46.5 %collective-permute-start.2 = (f32[1024,512]{0,1:T(8,128)}, f32[1024,512]{0,1:T(8,128)}, u32[]{:S(2)}, u32[]{:S(2)}) collective-permute-start(f32[1024,512]{0,1:T(8,128)} %all-reduce.2.cloned.1.call-done), channel_id=1, source_target_pairs={{0,1},{1,2},{2,3},{3,0},{4,5},{5,6},{6,7},{7,4},{8,9},{9,10},{10,1... | collective-permute-start | bytes 6291464 | tf_op jit(solution)/shard_map/ppermute | solution.py:19
  463.4 47.2 %collective-permute-start.3 = (f32[1024,512]{0,1:T(8,128)}, f32[1024,512]{0,1:T(8,128)}, u32[]{:S(2)}, u32[]{:S(2)}) collective-permute-start(f32[1024,512]{0,1:T(8,128)} %all-reduce.2.cloned.1.call-done), channel_id=1, source_target_pairs={{1,0},{2,1},{3,2},{0,3},{5,4},{6,5},{7,6},{4,7},{9,8},{10,9},{11,1... | collective-permute-start | bytes 6291464 | tf_op jit(solution)/shard_map/ppermute | solution.py:21
  466.3 44.3 %copy-start.3 = (f32[1024,512]{0,1:T(8,128)S(1)}, f32[1024,512]{0,1:T(8,128)}, u32[]{:S(2)}) copy-start(f32[1024,512]{0,1:T(8,128)} %all-reduce.2.cloned.1.call-done) | copy-start | bytes 6291460
  703.3 79.1 %copy-start.1 = (f32[8,128,128]{2,1,0:T(8,128)S(1)}, f32[8,128,128]{2,1,0:T(8,128)}, u32[]{:S(2)}) copy-start(f32[8,128,128]{2,1,0:T(8,128)} %param.18) | copy-start | bytes 1572868
Sparse Core Ops, SparseCore 0:
  362.0 101.3 all-reduce.1
